TPU v7x, 512 devices: a whole 4x4x16 slice. The times are simulated.
512 devices in a mesh: grp: 64 (over y_lo, z, core), tp: 8 (over x, y_hi).
Axes of the slice: x: 4, y: 4 (y_hi: 2, y_lo: 2; y = y_hi * 2 + y_lo), z: 16, core: 2. Of those that a mesh axis runs over, the one named last changes fastest.
Arguments:
- queries: bfloat16 [64, 2, 512, 2048], P('grp', None, None, 'tp'), may hold values from -9 to 9
- fresh_kv: bfloat16 [64, 2, 512, 2, 2048], P('grp', None, None, None, 'tp'), may hold values from -9 to 9
- stale_kv: bfloat16 [64, 2, 512, 2, 2048], P('grp', None, None, None, 'tp'), may hold values from -6 to 6
- text_kv: bfloat16 [64, 2, 256, 2, 2048], P('grp', None, None, None, 'tp'), may hold values from -6 to 6
- w_velocity: bfloat16 [2048, 64], P('tp'), may hold values from -2.390625 to 2.390625
- latent: float32 [64, 2, 512, 64], P('grp', None, 'tp'), may hold values from -6 to 6
- live_counts: int32 [64, 2], replicated, may hold values from 128 to 512, as said below
- refresh_rows: int32 [64, 2, 64], replicated, may hold values from 0 to 511, as said below
- request_list: int32 [64], replicated, may hold values from 0 to 63, each once
- timesteps: int32 [64, 2], replicated, may hold values from 0 to 999, as said below
Outputs:
- next_stale: bfloat16 [64, 2, 512, 2, 2048], P('grp', None, None, None, 'tp')
- velocity: float32 [64, 2, 512, 64], P('grp', None, 'tp')
- latent_next: float32 [64, 2, 512, 64], P('grp', None, 'tp')
Inputs may be any that keep to these rules, and one draw needn't show every extreme that they name: `live_counts`: 512 is reached in every draw. `refresh_rows`: rows within one list are distinct. `timesteps`: the next timestep is below the current one. `request_list`: each request appears once.
All inputs are finite; a program needn't handle non-finite values.
Results may differ from a plain program's by a relative error of at most 0.0045.
Values may be sent and summed in bfloat16 or wider, within the bound.
A program may use at most 64 MiB of HBM per device.

v0:
```python
import math
import jax
import jax.numpy as jnp
from jax import lax
from jax.sharding import PartitionSpec as P

HD = 128


def from_behind(block, axis, distance):
    devices = range(lax.axis_size(axis))
    route = [((i - distance) % len(devices), i) for i in devices]
    return lax.ppermute(block, axis, route)


def slot_velocity(slot_query, own_kv, partner_kv, text_pair, own_live, partner_live, w_velocity):
    img_rows = slot_query.shape[0]
    heads_here = slot_query.shape[1] // HD
    key_rows = jnp.concatenate([own_kv[:, 0], partner_kv[:, 0], text_pair[:, 0]], axis=0)
    value_rows = jnp.concatenate([own_kv[:, 1], partner_kv[:, 1], text_pair[:, 1]], axis=0)
    row_ids = jnp.arange(img_rows, dtype=jnp.int32)
    live_mask = jnp.concatenate(
        [row_ids < own_live, row_ids < partner_live, jnp.ones((text_pair.shape[0],), dtype=bool)]
    )
    outputs = []
    for head_index in range(heads_here):
        first = head_index * HD
        scores = lax.dot_general(
            slot_query[:, first : first + HD],
            key_rows[:, first : first + HD],
            (((1,), (1,)), ((), ())),
            preferred_element_type=jnp.float32,
        ) * (1.0 / math.sqrt(HD))
        scores = jnp.where(live_mask[None, :], scores, -jnp.inf)
        row_top = jnp.max(scores, axis=1, keepdims=True)
        weights = jnp.exp(scores - row_top)
        totals = jnp.sum(weights, axis=1, keepdims=True)
        blended = (
            jnp.dot(
                weights.astype(jnp.bfloat16),
                value_rows[:, first : first + HD],
                preferred_element_type=jnp.float32,
            )
            / totals
        )
        outputs.append(blended.astype(jnp.bfloat16))
    blended = jnp.concatenate(outputs, axis=1)
    return jnp.dot(blended, w_velocity, preferred_element_type=jnp.float32)


def shards(
    queries,
    fresh_kv,
    stale_kv,
    text_kv,
    w_velocity,
    latent,
    live_counts,
    refresh_rows,
    request_list,
    timesteps,
):
    groups_count = lax.axis_size("grp")
    half_groups = groups_count // 2
    my_group = lax.axis_index("grp")
    partner = (my_group + half_groups) % groups_count
    slot_count = queries.shape[1]
    partner_fresh = from_behind(fresh_kv, "grp", half_groups)
    text_other = from_behind(text_kv, "grp", half_groups)
    partner_lists = lax.dynamic_index_in_dim(refresh_rows, partner, 0, keepdims=False)
    my_live = lax.dynamic_index_in_dim(live_counts, my_group, 0, keepdims=False)
    partner_live = lax.dynamic_index_in_dim(live_counts, partner, 0, keepdims=False)
    arrived = jnp.stack(
        [
            jnp.take(partner_fresh[0, slot_index], partner_lists[slot_index], axis=0)
            for slot_index in range(slot_count)
        ]
    )
    partials = []
    for slot_index in range(slot_count):
        repaired = stale_kv[0, slot_index].at[partner_lists[slot_index]].set(arrived[slot_index])
        text_pair = jnp.concatenate([text_kv[0, slot_index], text_other[0, slot_index]], axis=0)
        partials.append(
            slot_velocity(
                queries[0, slot_index],
                fresh_kv[0, slot_index],
                repaired,
                text_pair,
                my_live[slot_index],
                partner_live[slot_index],
                w_velocity,
            )
        )
    partial_value = jnp.stack(partials)
    tp_count = lax.axis_size("tp")
    share = partial_value.shape[1] // tp_count
    tp_index = lax.axis_index("tp")
    whole = lax.psum(partial_value, "tp")
    summed = lax.dynamic_slice_in_dim(whole, tp_index * share, share, 1)
    row_ids = tp_index * share + jnp.arange(share, dtype=jnp.int32)
    live_rows = row_ids[None, :] < my_live[:, None]
    velocity = jnp.where(live_rows[:, :, None], summed, 0.0)
    pair_index = my_group % half_groups
    request_ids = lax.dynamic_slice_in_dim(request_list, pair_index * slot_count, slot_count)
    matches = (
        request_ids[:, None] == jnp.arange(timesteps.shape[0], dtype=jnp.int32)[None, :]
    ).astype(jnp.int32)
    times = jnp.dot(matches, timesteps)
    step_size = (times[:, 1] - times[:, 0]).astype(jnp.float32) / 1000.0
    latent_next = latent[0] + step_size[:, None, None] * velocity
    return (partner_fresh, velocity[None], latent_next[None])


def solution(mesh):
    return jax.shard_map(
        shards,
        mesh=mesh,
        in_specs=(
            P("grp", None, None, "tp"),
            P("grp", None, None, None, "tp"),
            P("grp", None, None, None, "tp"),
            P("grp", None, None, None, "tp"),
            P("tp", None),
            P("grp", None, "tp", None),
            P(),
            P(),
            P(),
            P(),
        ),
        out_specs=(
            P("grp", None, None, None, "tp"),
            P("grp", None, "tp", None),
            P("grp", None, "tp", None),
        ),
        check_vma=False,
    )
```

profile of v0, /device:TPU:32, one launch (start us, length us, event | category | flops | bytes accessed | tf_op | source)
XLA Modules:
  0.0 191.7 jit_solution(1452022395850017873)
XLA Ops:
  7.3 1.2 copy.61
  8.5 3.5 %collective-permute-start.1 = (bf16[1,2,256,2,256]{4,2,3,1,0:T(8,128)(2,1)S(1)}, bf16[1,2,256,2,256]{4,2,3,1,0:T(8,128)(2,1)}, u32[]{:S(2)}, u32[]{:S(2)}) collective-permute-start(bf16[1,2,256,2,256]{4,2,3,1,0:T(8,128)(2,1)S(1)} %copy.61), channel_id=1, source_target_pairs={{256,0},{264,8},{272,16},{280,24},{288,32},{296,40},{304,48},{312,... | collective-permute-start | bytes 1572872 | tf_op jit(solution)/shard_map/ppermute | solution.py:13
  12.0 2.4 %collective-permute-start = (bf16[1,2,512,2,256]{4,3,2,1,0:T(2,128)(2,1)}, bf16[1,2,512,2,256]{4,3,2,1,0:T(2,128)(2,1)S(1)}, u32[]{:S(2)}, u32[]{:S(2)}) collective-permute-start(bf16[1,2,512,2,256]{4,3,2,1,0:T(2,128)(2,1)} %param.13), channel_id=1, source_target_pairs={{256,0},{264,8},{272,16},{280,24},{288,32},{296,40},{304,48},{312,... | collective-permute-start | bytes 3145736 | tf_op jit(solution)/shard_map/ppermute | solution.py:13
  15.4 0.8 slice_bitcast_fusion.10
  16.3 1.9 %fusion.83 = (bf16[1,1,512,2,256]{4,3,2,1,0:T(2,128)(2,1)S(1)}, bf16[1,1,512,2,256]{4,3,2,1,0:T(2,128)(2,1)S(1)}) fusion(bf16[1,2,512,2,256]{4,3,2,1,0:T(2,128)(2,1)} %param.13), kind=kLoop, calls=%fused_computation.132 | loop fusion | bytes 2097152 | tf_op jit(solution)/shard_map/slice | solution.py:86
  18.5 0.8 multiply_reduce_fusion
  19.2 0.7 fusion.82
  22.4 0.8 slice_bitcast_fusion.13
  23.4 0.9 slice_bitcast_fusion.4
  24.2 0.7 iota_compare_fusion.2
  24.9 0.7 slice_bitcast_fusion.8
  25.7 2.7 %slice_bitcast_fusion.3 = (bf16[512,2,256]{2,1,0:T(2,128)(2,1)S(1)}, bf16[512,2,256]{2,1,0:T(2,128)(2,1)}) fusion(bf16[1,2,512,2,256]{4,3,2,1,0:T(2,128)(2,1)} %param.14), kind=kLoop, calls=%fused_computation.55 | loop fusion | bytes 2097152 | tf_op jit(solution)/shard_map/squeeze | solution.py:81
  28.4 1.1 slice_bitcast_fusion.9
  29.5 0.9 fusion.60
  30.4 16.1 %collective-permute-done = bf16[1,2,512,2,256]{4,3,2,1,0:T(2,128)(2,1)S(1)} collective-permute-done((bf16[1,2,512,2,256]{4,3,2,1,0:T(2,128)(2,1)}, bf16[1,2,512,2,256]{4,3,2,1,0:T(2,128)(2,1)S(1)}, u32[]{:S(2)}, u32[]{:S(2)}) %collective-permute-start) | collective-permute-done | bytes 1048608 | tf_op jit(solution)/shard_map/ppermute | solution.py:13
  46.5 1.5 slice_bitcast_fusion.1
  48.0 1.8 gather_fusion
  49.8 0.7 gather_fusion.1
  50.5 0.9 broadcast_select_fusion
  51.4 2.6 %scatter_fusion = bf16[512,2,256]{2,1,0:T(2,128)(2,1)S(1)} fusion(bf16[512,2,256]{2,1,0:T(2,128)(2,1)S(1)} %get-tuple-element.32, s32[64]{0:T(128)S(1)} %get-tuple-element.56, bf16[64,2,256]{2,1,0:T(2,128)(2,1)S(1)} %get-tuple-element.78), kind=kCustom, calls=%fused_computation.2 | custom fusion | bytes 196864 | tf_op jit(solution)/shard_map/scatter | solution.py:81
  54.0 1.5 fusion.84
  55.7 2.2 %fusion.90 = (f32[512]{0:T(512)S(1)}, f32[1536,512]{1,0:T(8,128)}) fusion(bf16[512,256]{1,0:T(8,128)(2,1)S(1)} %copy-done.5, bf16[1536,256]{1,0:T(8,128)(2,1)S(1)} %pad_maximum_fusion, pred[1536]{0:T(1024)(128)(4,1)S(1)} %get-tuple-element.63), kind=kOutput, calls=%fused_computation.139 | convolution fusion | flops 203685376 | bytes 3674112 | tf_op jit(solution)/shard_map/dot_general | solution.py:28
  58.5 7.5 %scatter_fusion.1 = bf16[512,2,256]{2,1,0:T(2,128)(2,1)} fusion(bf16[512,2,256]{2,1,0:T(2,128)(2,1)} %get-tuple-element.33, s32[64]{0:T(128)} %get-tuple-element.57, bf16[64,2,256]{2,1,0:T(2,128)(2,1)S(1)} %get-tuple-element.77), kind=kCustom, calls=%fused_computation.3 | custom fusion | bytes 196864 | tf_op jit(solution)/shard_map/scatter | solution.py:81
  66.0 2.1 %fusion.85 = (bf16[512,1,256]{2,1,0:T(2,128)(2,1)S(1)}, bf16[512,1,256]{2,1,0:T(2,128)(2,1)S(1)}) fusion(bf16[512,2,256]{2,1,0:T(2,128)(2,1)} %scatter_fusion.1), kind=kLoop, calls=%fused_computation.134 | loop fusion | bytes 1048576 | tf_op jit(solution)/shard_map/slice | solution.py:20
  68.2 1.1 pad_maximum_fusion.2
  70.9 1.0 copy-done.1
  76.9 0.7 pad_maximum_fusion.6
  77.8 103.7 %all-reduce.2.cloned.1.call-done = f32[2,512,64]{1,2,0:T(8,128)} async-done(((f32[2,512,64]{1,2,0:T(8,128)}), f32[2,512,64]{1,2,0:T(8,128)}) %all-reduce.2.cloned.1.call-update) | async-done | bytes 262160 | tf_op jit(solution)/shard_map/psum | solution.py:98
  181.5 0.9 fusion.72
  182.5 0.7 copy.67
  183.2 0.7 copy.66
  183.9 1.0 copy.88
  (81 shorter events, 11.4 us)
Async XLA Ops:
  7.2 7.2 %copy-start = (s32[64,2,64]{2,1,0:T(2,128)S(1)}, s32[64,2,64]{2,1,0:T(2,128)}, u32[]{:S(2)}) copy-start(s32[64,2,64]{2,1,0:T(2,128)} %param.19) | copy-start | bytes 98308
  7.2 11.0 %copy-start.20 = (s32[64]{0:T(128)S(1)}, s32[64]{0:T(128)}, u32[]{:S(2)}) copy-start(s32[64]{0:T(128)} %param.20) | copy-start | bytes 772
  7.2 11.1 %copy-start.19 = (s32[64,2]{0,1:T(2,128)S(1)}, s32[64,2]{0,1:T(2,128)}, u32[]{:S(2)}) copy-start(s32[64,2]{0,1:T(2,128)} %param.21) | copy-start | bytes 1540
  7.2 12.0 %copy-start.15 = (s32[64,2]{0,1:T(2,128)S(1)}, s32[64,2]{0,1:T(2,128)}, u32[]{:S(2)}) copy-start(s32[64,2]{0,1:T(2,128)} %param.18) | copy-start | bytes 1540
  7.2 15.2 %copy-start.13 = (bf16[1,2,512,256]{3,2,1,0:T(8,128)(2,1)S(1)}, bf16[1,2,512,256]{3,2,1,0:T(8,128)(2,1)}, u32[]{:S(2)}) copy-start(bf16[1,2,512,256]{3,2,1,0:T(8,128)(2,1)} %param.12) | copy-start | bytes 1572868
  7.2 174.3 %all-reduce.2.cloned.1.call-start = ((), (), s32[]{:S(2)}) async-start(), calls=%async_computation | async-start | bytes 524288 | tf_op jit(solution)/shard_map/psum | solution.py:98
  8.5 20.0 %collective-permute-start.1 = (bf16[1,2,256,2,256]{4,2,3,1,0:T(8,128)(2,1)S(1)}, bf16[1,2,256,2,256]{4,2,3,1,0:T(8,128)(2,1)}, u32[]{:S(2)}, u32[]{:S(2)}) collective-permute-start(bf16[1,2,256,2,256]{4,2,3,1,0:T(8,128)(2,1)S(1)} %copy.61), channel_id=1, source_target_pairs={{256,0},{264,8},{272,16},{280,24},{288,32},{296,40},{304,48},{312,... | collective-permute-start | bytes 1572872 | tf_op jit(solution)/shard_map/ppermute | solution.py:13
  12.0 34.5 %collective-permute-start = (bf16[1,2,512,2,256]{4,3,2,1,0:T(2,128)(2,1)}, bf16[1,2,512,2,256]{4,3,2,1,0:T(2,128)(2,1)S(1)}, u32[]{:S(2)}, u32[]{:S(2)}) collective-permute-start(bf16[1,2,512,2,256]{4,3,2,1,0:T(2,128)(2,1)} %param.13), channel_id=1, source_target_pairs={{256,0},{264,8},{272,16},{280,24},{288,32},{296,40},{304,48},{312,... | collective-permute-start | bytes 3145736 | tf_op jit(solution)/shard_map/ppermute | solution.py:13
  23.3 6.2 %copy-start.10 = (bf16[256,2,256]{2,0,1:T(8,128)(2,1)S(1)}, bf16[256,2,256]{2,0,1:T(8,128)(2,1)}, u32[]{:S(2)}) copy-start(bf16[256,2,256]{2,0,1:T(8,128)(2,1)} %get-tuple-element.44) | copy-start | bytes 786436
  23.4 6.2 %copy-start.11 = (bf16[256,2,256]{2,0,1:T(8,128)(2,1)S(1)}, bf16[256,2,256]{2,0,1:T(8,128)(2,1)}, u32[]{:S(2)}) copy-start(bf16[256,2,256]{2,0,1:T(8,128)(2,1)} %get-tuple-element.45) | copy-start | bytes 786436
  30.4 25.2 %copy-start.5 = (bf16[512,256]{1,0:T(8,128)(2,1)S(1)}, bf16[512,256]{1,0:T(8,128)(2,1)}, u32[]{:S(2)}) copy-start(bf16[512,256]{1,0:T(8,128)(2,1)} %get-tuple-element.40) | copy-start | bytes 786436
  46.5 9.2 %copy-start.2 = (bf16[1,2,512,2,256]{4,3,2,1,0:T(2,128)(2,1)}, bf16[1,2,512,2,256]{4,3,2,1,0:T(2,128)(2,1)S(1)}, u32[]{:S(2)}) copy-start(bf16[1,2,512,2,256]{4,3,2,1,0:T(2,128)(2,1)S(1)} %collective-permute-done) | copy-start | bytes 3145732
  55.5 2.3 %copy-start.6 = (bf16[512,256]{1,0:T(8,128)(2,1)S(1)}, bf16[512,256]{1,0:T(8,128)(2,1)}, u32[]{:S(2)}) copy-start(bf16[512,256]{1,0:T(8,128)(2,1)} %get-tuple-element.40) | copy-start | bytes 786436
  69.8 1.0 copy-start.4
  69.8 2.1 %copy-start.1 = (f32[1536,512]{1,0:T(8,128)S(1)}, f32[1536,512]{1,0:T(8,128)}, u32[]{:S(2)}) copy-start(f32[1536,512]{1,0:T(8,128)} %get-tuple-element.70) | copy-start | bytes 9437188
  70.5 1.9 %copy-start.8 = (bf16[512,256]{1,0:T(8,128)(2,1)S(1)}, bf16[512,256]{1,0:T(8,128)(2,1)}, u32[]{:S(2)}) copy-start(bf16[512,256]{1,0:T(8,128)(2,1)} %get-tuple-element.34) | copy-start | bytes 786436
  70.5 1.9 %copy-start.12 = (bf16[512,256]{1,0:T(8,128)(2,1)S(1)}, bf16[512,256]{1,0:T(8,128)(2,1)}, u32[]{:S(2)}) copy-start(bf16[512,256]{1,0:T(8,128)(2,1)} %get-tuple-element.76) | copy-start | bytes 786436
  73.6 1.1 copy-start.7
  73.6 1.1 copy-start.9
  75.4 1.2 copy-start.18
  75.9 1.8 copy-start.14
  75.9 1.9 copy-start.17
  75.9 105.6 %copy-start.16 = (f32[2]{0:T(128)S(1)}, f32[2]{0:T(128)}, u32[]{:S(2)}) copy-start(f32[2]{0:T(128)} %multiply_reduce_fusion) | copy-start | bytes 28
  75.9 108.0 %copy-start.3 = (bf16[1,2,512,2,256]{4,3,2,1,0:T(2,128)(2,1)S(1)}, bf16[1,2,512,2,256]{4,3,2,1,0:T(2,128)(2,1)}, u32[]{:S(2)}) copy-start(bf16[1,2,512,2,256]{4,3,2,1,0:T(2,128)(2,1)} %copy-done.2) | copy-start | bytes 3145732
Sparse Core Ops, SparseCore 0:
  77.8 103.7 all-reduce.1
where the time goes:
time: 192 us
  waiting for transfers between devices  120 us (62%)
  local copies, waits for them, and re-layouts  33.5 us (17%)
  between operations  14.5 us (8%)
  other arithmetic  11.1 us (6%)
  matrix products  6.91 us (4%)
  starting transfers between devices  5.88 us (3%)
    psum x1, waiting for transfers between devices, shards(): whole = lax.psum(partial_value, 'tp')  104 us
    ppermute x2, waiting for transfers between devices, from_behind(): return lax.ppermute(block, axis, route)  16.1 us
    scatter x2, local copies, waits for them, and re-layouts, shards(): stale_kv[0, slot_index].at[partner_lists[slot_index]]  10.2 us
    ppermute x2, starting transfers between devices, from_behind(): return lax.ppermute(block, axis, route)  5.85 us
    unnamed x51, local copies, waits for them, and re-layouts  5.25 us
    dot_general x4, matrix products, slot_velocity(): lax.dot_general(slot_query[:, first:first + HD], key_rows[:, first:first...  3.98 us
  transfers between devices with their start and end apart: 3, of which 2 were waited for; matrix products, arithmetic and copies ran while one was open for 8% of the time, Pallas kernels for 0%

commit v1 on v0

--- a/solution.py
+++ b/solution.py
@@ -95,7 +95,7 @@
     tp_count = lax.axis_size("tp")
     share = partial_value.shape[1] // tp_count
     tp_index = lax.axis_index("tp")
-    whole = lax.psum(partial_value, "tp")
+    whole = jnp.sum(lax.all_gather(partial_value, "tp"), axis=0)
     summed = lax.dynamic_slice_in_dim(whole, tp_index * share, share, 1)
     row_ids = tp_index * share + jnp.arange(share, dtype=jnp.int32)
     live_rows = row_ids[None, :] < my_live[:, None]

time: 192 us -> 165 us (0.86)
  the two profiles are of different devices: /device:TPU:32 before, /device:TPU:2 now
where the time goes in v1:
time: 165 us; the launch traced here: 164 us
  waiting for transfers between devices  92 us (56%)
  local copies, waits for them, and re-layouts  32.4 us (20%)
  between operations  14.5 us (9%)
  other arithmetic  11.7 us (7%)
  matrix products  7.82 us (5%)
  starting transfers between devices  5.88 us (4%)
    all_gather x1, waiting for transfers between devices, shards(): whole = jnp.sum(lax.all_gather(partial_value, 'tp'), axis=0)  74 us
    ppermute x2, waiting for transfers between devices, from_behind(): return lax.ppermute(block, axis, route)  17.9 us
    scatter x2, local copies, waits for them, and re-layouts, shards(): stale_kv[0, slot_index].at[partner_lists[slot_index]]  10.2 us
    ppermute x2, starting transfers between devices, from_behind(): return lax.ppermute(block, axis, route)  5.85 us
    unnamed x47, local copies, waits for them, and re-layouts  5.18 us
    dot_general x4, matrix products, slot_velocity(): lax.dot_general(slot_query[:, first:first + HD], key_rows[:, first:first...  4.89 us
    slice x2, local copies, waits for them, and re-layouts, slot_velocity(): partner_kv[:, 1]  3.61 us
  transfers between devices with their start and end apart: 3, of which 2 were waited for; matrix products, arithmetic and copies ran while one was open for 9% of the time, Pallas kernels for 0%

profile of v1, /device:TPU:2, one launch (start us, length us, event | category | flops | bytes accessed | tf_op | source)
XLA Modules:
  0.0 164.3 jit_solution(16635053077995460322)
XLA Ops:
  7.2 1.1 copy.51
  8.4 3.5 %collective-permute-start.1 = (bf16[1,2,256,2,256]{4,2,3,1,0:T(8,128)(2,1)S(1)}, bf16[1,2,256,2,256]{4,2,3,1,0:T(8,128)(2,1)}, u32[]{:S(2)}, u32[]{:S(2)}) collective-permute-start(bf16[1,2,256,2,256]{4,2,3,1,0:T(8,128)(2,1)S(1)} %copy.51), channel_id=1, source_target_pairs={{256,0},{264,8},{272,16},{280,24},{288,32},{296,40},{304,48},{312,... | collective-permute-start | bytes 1572872 | tf_op jit(solution)/shard_map/ppermute | solution.py:13
  11.8 2.4 %collective-permute-start = (bf16[1,2,512,2,256]{4,3,2,1,0:T(2,128)(2,1)}, bf16[1,2,512,2,256]{4,3,2,1,0:T(2,128)(2,1)S(1)}, u32[]{:S(2)}, u32[]{:S(2)}) collective-permute-start(bf16[1,2,512,2,256]{4,3,2,1,0:T(2,128)(2,1)} %param.13), channel_id=1, source_target_pairs={{256,0},{264,8},{272,16},{280,24},{288,32},{296,40},{304,48},{312,... | collective-permute-start | bytes 3145736 | tf_op jit(solution)/shard_map/ppermute | solution.py:13
  15.3 0.7 slice_bitcast_fusion.10
  16.0 1.9 %fusion.83 = (bf16[1,1,512,2,256]{4,3,2,1,0:T(2,128)(2,1)S(1)}, bf16[1,1,512,2,256]{4,3,2,1,0:T(2,128)(2,1)S(1)}) fusion(bf16[1,2,512,2,256]{4,3,2,1,0:T(2,128)(2,1)} %param.13), kind=kLoop, calls=%fused_computation.132 | loop fusion | bytes 2097152 | tf_op jit(solution)/shard_map/slice | solution.py:86
  18.0 0.8 fusion.82
  20.6 0.7 iota_compare_fusion
  21.3 1.1 slice_bitcast_fusion.13
  22.6 0.8 slice_bitcast_fusion.4
  24.1 0.7 slice_bitcast_fusion.8
  24.8 1.5 slice_bitcast_fusion.3
  26.4 1.1 slice_bitcast_fusion.9
  27.4 1.0 fusion.60
  28.4 17.9 %collective-permute-done = bf16[1,2,512,2,256]{4,3,2,1,0:T(2,128)(2,1)S(1)} collective-permute-done((bf16[1,2,512,2,256]{4,3,2,1,0:T(2,128)(2,1)}, bf16[1,2,512,2,256]{4,3,2,1,0:T(2,128)(2,1)S(1)}, u32[]{:S(2)}, u32[]{:S(2)}) %collective-permute-start) | collective-permute-done | bytes 1048608 | tf_op jit(solution)/shard_map/ppermute | solution.py:13
  46.4 1.5 slice_bitcast_fusion.1
  47.9 1.8 %gather_fusion = bf16[64,2,256]{2,1,0:T(2,128)(2,1)S(1)} fusion(bf16[512,2,256]{2,1,0:T(2,128)(2,1)} %get-tuple-element.15, s32[1024]{0:T(1024)S(1)} %pad_clamp_fusion.1), kind=kCustom, calls=%fused_computation.clone | custom fusion | bytes 131328 | tf_op jit(solution)/shard_map/jit(_take)/gather | solution.py:75
  49.7 0.7 gather_fusion.1
  50.4 0.9 broadcast_select_fusion
  51.3 2.6 %scatter_fusion = bf16[512,2,256]{2,1,0:T(2,128)(2,1)S(1)} fusion(bf16[512,2,256]{2,1,0:T(2,128)(2,1)S(1)} %get-tuple-element.17, s32[64]{0:T(128)S(1)} %get-tuple-element.41, bf16[64,2,256]{2,1,0:T(2,128)(2,1)S(1)} %get-tuple-element.63), kind=kCustom, calls=%fused_computation.2 | custom fusion | bytes 196864 | tf_op jit(solution)/shard_map/scatter | solution.py:81
  53.9 1.5 fusion.84
  55.6 2.2 %fusion.90 = (f32[512]{0:T(512)S(1)}, f32[1536,512]{1,0:T(8,128)}) fusion(bf16[512,256]{1,0:T(8,128)(2,1)S(1)} %get-tuple-element.25, bf16[1536,256]{1,0:T(8,128)(2,1)S(1)} %pad_maximum_fusion, pred[1536]{0:T(1024)(128)(4,1)S(1)} %get-tuple-element.48), kind=kOutput, calls=%fused_computation.139 | convolution fusion | flops 203685376 | bytes 3674112 | tf_op jit(solution)/shard_map/dot_general | solution.py:28
  57.8 1.5 fusion.91
  59.3 7.5 %scatter_fusion.1 = bf16[512,2,256]{2,1,0:T(2,128)(2,1)} fusion(bf16[512,2,256]{2,1,0:T(2,128)(2,1)} %get-tuple-element.18, s32[64]{0:T(128)} %get-tuple-element.42, bf16[64,2,256]{2,1,0:T(2,128)(2,1)S(1)} %get-tuple-element.62), kind=kCustom, calls=%fused_computation.3 | custom fusion | bytes 196864 | tf_op jit(solution)/shard_map/scatter | solution.py:81
  66.8 2.1 %fusion.85 = (bf16[512,1,256]{2,1,0:T(2,128)(2,1)S(1)}, bf16[512,1,256]{2,1,0:T(2,128)(2,1)S(1)}) fusion(bf16[512,2,256]{2,1,0:T(2,128)(2,1)} %scatter_fusion.1), kind=kLoop, calls=%fused_computation.134 | loop fusion | bytes 1048576 | tf_op jit(solution)/shard_map/slice | solution.py:20
  68.9 1.1 pad_maximum_fusion.2
  71.7 1.0 copy-done.1
  77.7 0.7 pad_maximum_fusion.6
  79.1 74.0 %all-gather.3.cloned.1.call-done = f32[16,512,64]{1,2,0:T(8,128)} async-done(((f32[2,512,64]{1,2,0:T(8,128)}), f32[16,512,64]{1,2,0:T(8,128)}) %all-gather.3.cloned.1.call-update) | async-done | bytes 2097168 | tf_op jit(solution)/shard_map/all_gather | solution.py:98
  153.1 1.8 %reduce_sum.49 = f32[2,512,64]{1,2,0:T(8,128)S(1)} reduce(f32[8,2,512,64]{2,3,1,0:T(8,128)} %bitcast.88, f32[]{:T(128)} %constant.66.clone.1), dimensions={0}, to_apply=%region_10.12 | reduce | flops 458752 | bytes 2359300 | tf_op jit(solution)/shard_map/reduce_sum | solution.py:98
  155.0 0.7 copy.57
  155.7 0.7 copy.56
  156.5 1.0 copy.77
  (78 shorter events, 11.2 us)
Async XLA Ops:
  7.2 7.1 %copy-start = (s32[64,2,64]{2,1,0:T(2,128)S(1)}, s32[64,2,64]{2,1,0:T(2,128)}, u32[]{:S(2)}) copy-start(s32[64,2,64]{2,1,0:T(2,128)} %param.19) | copy-start | bytes 98308
  7.2 10.8 %copy-start.14 = (s32[64,2]{0,1:T(2,128)S(1)}, s32[64,2]{0,1:T(2,128)}, u32[]{:S(2)}) copy-start(s32[64,2]{0,1:T(2,128)} %param.18) | copy-start | bytes 1540
  7.2 145.9 %all-gather.3.cloned.1.call-start = ((), (), s32[]{:S(2)}) async-start(), calls=%async_computation | async-start | bytes 2359296 | tf_op jit(solution)/shard_map/all_gather | solution.py:98
  8.4 18.0 %collective-permute-start.1 = (bf16[1,2,256,2,256]{4,2,3,1,0:T(8,128)(2,1)S(1)}, bf16[1,2,256,2,256]{4,2,3,1,0:T(8,128)(2,1)}, u32[]{:S(2)}, u32[]{:S(2)}) collective-permute-start(bf16[1,2,256,2,256]{4,2,3,1,0:T(8,128)(2,1)S(1)} %copy.51), channel_id=1, source_target_pairs={{256,0},{264,8},{272,16},{280,24},{288,32},{296,40},{304,48},{312,... | collective-permute-start | bytes 1572872 | tf_op jit(solution)/shard_map/ppermute | solution.py:13
  11.8 34.5 %collective-permute-start = (bf16[1,2,512,2,256]{4,3,2,1,0:T(2,128)(2,1)}, bf16[1,2,512,2,256]{4,3,2,1,0:T(2,128)(2,1)S(1)}, u32[]{:S(2)}, u32[]{:S(2)}) collective-permute-start(bf16[1,2,512,2,256]{4,3,2,1,0:T(2,128)(2,1)} %param.13), channel_id=1, source_target_pairs={{256,0},{264,8},{272,16},{280,24},{288,32},{296,40},{304,48},{312,... | collective-permute-start | bytes 3145736 | tf_op jit(solution)/shard_map/ppermute | solution.py:13
  18.0 6.9 %copy-start.5 = (bf16[1,2,512,2,256]{4,3,2,1,0:T(2,128)(2,1)S(1)}, bf16[1,2,512,2,256]{4,3,2,1,0:T(2,128)(2,1)}, u32[]{:S(2)}) copy-start(bf16[1,2,512,2,256]{4,3,2,1,0:T(2,128)(2,1)} %param.14) | copy-start | bytes 3145732
  22.4 33.1 %copy-start.6 = (bf16[512,256]{1,0:T(8,128)(2,1)}, bf16[512,256]{1,0:T(8,128)(2,1)S(1)}, u32[]{:S(2)}) copy-start(bf16[512,256]{1,0:T(8,128)(2,1)S(1)} %get-tuple-element.25) | copy-start | bytes 786436
  22.6 4.9 %copy-start.11 = (bf16[256,2,256]{2,0,1:T(8,128)(2,1)S(1)}, bf16[256,2,256]{2,0,1:T(8,128)(2,1)}, u32[]{:S(2)}) copy-start(bf16[256,2,256]{2,0,1:T(8,128)(2,1)} %get-tuple-element.30) | copy-start | bytes 786436
  28.4 27.0 %copy-start.12 = (bf16[512,256]{1,0:T(8,128)(2,1)S(1)}, bf16[512,256]{1,0:T(8,128)(2,1)}, u32[]{:S(2)}) copy-start(bf16[512,256]{1,0:T(8,128)(2,1)} %get-tuple-element.60) | copy-start | bytes 786436
  46.4 9.2 %copy-start.2 = (bf16[1,2,512,2,256]{4,3,2,1,0:T(2,128)(2,1)}, bf16[1,2,512,2,256]{4,3,2,1,0:T(2,128)(2,1)S(1)}, u32[]{:S(2)}) copy-start(bf16[1,2,512,2,256]{4,3,2,1,0:T(2,128)(2,1)S(1)} %collective-permute-done) | copy-start | bytes 3145732
  70.6 1.0 copy-start.4
  70.6 2.1 %copy-start.1 = (f32[1536,512]{1,0:T(8,128)S(1)}, f32[1536,512]{1,0:T(8,128)}, u32[]{:S(2)}) copy-start(f32[1536,512]{1,0:T(8,128)} %get-tuple-element.55) | copy-start | bytes 9437188
  71.2 1.9 %copy-start.8 = (bf16[512,256]{1,0:T(8,128)(2,1)S(1)}, bf16[512,256]{1,0:T(8,128)(2,1)}, u32[]{:S(2)}) copy-start(bf16[512,256]{1,0:T(8,128)(2,1)} %get-tuple-element.19) | copy-start | bytes 786436
  71.2 1.9 %copy-start.10 = (bf16[512,256]{1,0:T(8,128)(2,1)S(1)}, bf16[512,256]{1,0:T(8,128)(2,1)}, u32[]{:S(2)}) copy-start(bf16[512,256]{1,0:T(8,128)(2,1)} %get-tuple-element.61) | copy-start | bytes 786436
  74.4 1.1 copy-start.7
  74.4 1.1 copy-start.9
  76.2 1.2 copy-start.16
  76.7 1.8 %copy-start.13 = (f32[1,2,64,64]{3,2,1,0:T(8,128)S(1)}, f32[1,2,64,64]{3,2,1,0:T(8,128)}, u32[]{:S(2)}) copy-start(f32[1,2,64,64]{3,2,1,0:T(8,128)} %param.17) | copy-start | bytes 98308
  76.7 1.9 %copy-start.18 = (s32[64]{0:T(128)S(1)}, s32[64]{0:T(128)}, u32[]{:S(2)}) copy-start(s32[64]{0:T(128)} %param.20) | copy-start | bytes 772
  76.7 1.9 %copy-start.17 = (s32[64,2]{0,1:T(2,128)S(1)}, s32[64,2]{0,1:T(2,128)}, u32[]{:S(2)}) copy-start(s32[64,2]{0,1:T(2,128)} %param.21) | copy-start | bytes 1540
  76.7 2.3 %copy-start.15 = (s32[2]{0:T(128)S(1)}, s32[2]{0:T(128)}, u32[]{:S(2)}) copy-start(s32[2]{0:T(128)} %get-tuple-element.7) | copy-start | bytes 28
  77.3 79.1 %copy-start.3 = (bf16[1,2,512,2,256]{4,3,2,1,0:T(2,128)(2,1)S(1)}, bf16[1,2,512,2,256]{4,3,2,1,0:T(2,128)(2,1)}, u32[]{:S(2)}) copy-start(bf16[1,2,512,2,256]{4,3,2,1,0:T(2,128)(2,1)} %copy-done.2) | copy-start | bytes 3145732
Sparse Core Ops, SparseCore 0:
  78.6 74.5 all-gather.2
